TPU v7x, 256 devices: a whole 4x4x8 slice. The times are simulated.
256 devices in a mesh: ctx: 32 (over y, x, core), head: 8 (over z).
Axes of the slice: x: 4, y: 4, z: 8, core: 2. Of those that a mesh axis runs over, the one named last changes fastest.
Arguments:
- query_rows: bfloat16 [32768, 4096], P('ctx', 'head'), may hold values from -6 to 6
- key_rows: bfloat16 [32768, 4096], P('ctx', 'head'), may hold values from -6 to 6
- value_rows: bfloat16 [32768, 4096], P('ctx', 'head'), may hold values from -6 to 6
- frequencies: bfloat16 [32, 128, 128], P('head'), may hold values from -4.1875 to 4.1875
- norm_gain: bfloat16 [4096], P('head'), may hold values from 0.25 to 1.75
- out_weight: bfloat16 [4096, 4096], P(None, 'head'), may hold values from -0.09375 to 0.09375
Outputs:
- projected: bfloat16 [32768, 4096], P('ctx', 'head')
All inputs are finite; a program needn't handle non-finite values.
Results may differ from a plain program's by a relative error of at most 0.009.
Values may be sent and summed in bfloat16 or wider, within the bound.
A program may use at most 128 MiB of HBM per device.

v0:
```python
import math
import jax
import jax.numpy as jnp
from jax import lax
from jax.sharding import PartitionSpec as P


def carried_in(value, axis, join, neutral):
    count, mine = (lax.axis_size(axis), lax.axis_index(axis))
    pieces = lax.all_gather(value, axis)
    subtotal = jnp.full_like(value, 0) + jnp.asarray(neutral, value.dtype)

    def turn(position, subtotal):
        longer = join(subtotal, pieces[position])
        return jnp.where(position < mine, longer, subtotal)

    return lax.fori_loop(0, count - 1, turn, subtotal)


def features_of(inputs, frequencies, freq_count):
    phases = jnp.einsum("bthd,hdf->bthf", inputs, frequencies, preferred_element_type=jnp.float32)
    joined = jnp.concatenate([jnp.cos(phases), jnp.sin(phases)], axis=-1)
    return (joined * (1.0 / math.sqrt(freq_count))).astype(jnp.bfloat16)


def add_states(first_part, second_part):
    return first_part + second_part


def local(query_rows, key_rows, value_rows, frequencies, norm_gain, out_weight):
    row_count = query_rows.shape[0]
    heads_here, head_width, freq_count = frequencies.shape
    span_rows = min(512, row_count)
    span_count = row_count // span_rows
    span_shape = (span_count, span_rows, heads_here, head_width)
    query_spans = query_rows.reshape(span_shape)
    key_spans = key_rows.reshape(span_shape)
    value_spans = value_rows.reshape(span_shape)
    query_feat = features_of(query_spans, frequencies, freq_count)
    key_feat = features_of(key_spans, frequencies, freq_count)
    span_states = jnp.einsum(
        "bthf,bthd->bhfd", key_feat, value_spans, preferred_element_type=jnp.float32
    )
    shard_total = jnp.sum(span_states, axis=0)
    preceding = carried_in(shard_total, "ctx", add_states, jnp.zeros_like(shard_total))
    running_sums = jnp.cumsum(span_states, axis=0)
    earlier_local = jnp.concatenate([jnp.zeros_like(span_states[:1]), running_sums[:-1]], axis=0)
    carried_low = (preceding[None] + earlier_local).astype(jnp.bfloat16)
    causal = jnp.arange(span_rows)[:, None] >= jnp.arange(span_rows)[None, :]
    scores = jnp.einsum("bthf,bshf->bhts", query_feat, key_feat, preferred_element_type=jnp.float32)
    scores = jnp.where(causal[None, None], scores, jnp.zeros_like(scores)).astype(jnp.bfloat16)
    local_part = jnp.einsum(
        "bhts,bshd->bthd", scores, value_spans, preferred_element_type=jnp.float32
    )
    prior_part = jnp.einsum(
        "bthf,bhfd->bthd", query_feat, carried_low, preferred_element_type=jnp.float32
    )
    attended = local_part + prior_part
    gain_table = norm_gain.astype(jnp.float32).reshape(heads_here, head_width)
    mean_square = jnp.mean(attended * attended, axis=-1, keepdims=True)
    normed = (attended * lax.rsqrt(mean_square + 1e-06) * gain_table[None, None]).astype(
        jnp.bfloat16
    )
    normed = normed.reshape(row_count, heads_here * head_width)
    projected = jnp.dot(
        lax.all_gather(normed, "head", axis=1, tiled=True),
        out_weight,
        preferred_element_type=jnp.float32,
    )
    return projected.astype(jnp.bfloat16)


def solution(mesh):
    return jax.shard_map(
        local,
        mesh=mesh,
        in_specs=(
            P("ctx", "head"),
            P("ctx", "head"),
            P("ctx", "head"),
            P("head", None, None),
            P("head"),
            P(None, "head"),
        ),
        out_specs=P("ctx", "head"),
        check_vma=False,
    )
```

profile of v0, /device:TPU:1, one launch (start us, length us, event | category | flops | bytes accessed | tf_op | source)
XLA Modules:
  0.0 270.1 jit_solution(10711758108041598171)
XLA Ops:
  6.5 1.4 reshape.34
  8.4 9.7 %cosine_bitcast_fusion.1 = (f32[2,512,4,128]{1,3,0,2:T(8,128)}, f32[2,512,4,128]{1,3,0,2:T(8,128)}) fusion(bf16[2,512,4,128]{3,2,1,0:T(4,128)(2,1)S(1)} %reshape.34, bf16[4,128,128]{2,1,0:T(8,128)(2,1)S(1)} %copy-done), kind=kOutput, calls=%fused_computation.16 | convolution fusion | flops 134217728 | bytes 5373952 | tf_op jit(solution)/shard_map/bthd,hdf->bthf/dot_general | solution.py:21
  18.1 9.7 %cosine_bitcast_fusion = (f32[2,512,4,128]{1,3,0,2:T(8,128)}, f32[2,512,4,128]{1,3,0,2:T(8,128)}) fusion(bf16[2,512,4,128]{3,2,1,0:T(4,128)(2,1)S(1)} %reshape.35, bf16[4,128,128]{2,1,0:T(8,128)(2,1)S(1)} %copy-done), kind=kOutput, calls=%fused_computation.14 | convolution fusion | flops 134217728 | bytes 5373952 | tf_op jit(solution)/shard_map/bthd,hdf->bthf/dot_general | solution.py:21
  28.2 4.4 %fusion.1 = (bf16[2,512,4,256]{1,3,0,2:T(8,128)(2,1)S(1)}, bf16[2,512,4,256]{1,3,0,2:T(8,128)(2,1)S(1)}) fusion(f32[2,512,4,128]{1,3,0,2:T(8,128)} %get-tuple-element.109, f32[2,512,4,128]{1,3,0,2:T(8,128)} %get-tuple-element.108, f32[2,512,4,128]{1,3,0,2:T(8,128)} %get-tuple-element.111, f32[2,512,4,128]{1,3,0,2:T(8,128)} %get-tuple-element.110), kind=kLoop, calls=%fused_computation.4 | loop fusion | flops 6291456 | bytes 12582912 | tf_op jit(solution)/shard_map/convert_element_type | solution.py:23
  32.6 2.5 fusion.28
  35.2 1.3 fusion.37
  36.7 5.8 %fusion = f32[2,4,512,128]{2,3,1,0:T(8,128)} fusion(pred[512,512]{1,0:T(8,128)(4,1)S(1)} %iota_compare_fusion, bf16[2,512,4,256]{1,3,0,2:T(8,128)(2,1)} %copy-done.1, bf16[2,512,4,256]{1,3,0,2:T(8,128)(2,1)S(1)} %get-tuple-element.116, bf16[2,512,4,128]{3,2,1,0:T(4,128)(2,1)} %copy-done.4), kind=kOutput, calls=%fused_computation.2 | convolution fusion | flops 1614807040 | bytes 7602176 | tf_op jit(solution)/shard_map/bhts,bshd->bthd/dot_general | solution.py:52
  42.5 74.5 %all-gather.6.cloned.1.call-done = f32[128,256,128]{2,1,0:T(8,128)} async-done(((f32[4,256,128]{2,1,0:T(8,128)}), f32[128,256,128]{2,1,0:T(8,128)}) %all-gather.6.cloned.1.call-update) | async-done | bytes 16777232 | tf_op jit(solution)/shard_map/all_gather | solution.py:10
  117.0 38.4 %while.14 = (s32[]{:T(128)}, f32[4,256,128]{2,1,0:T(8,128)S(1)}, s32[]{:T(128)}, f32[32,4,256,128]{3,2,1,0:T(8,128)}, s32[]{:T(128)}, /*index=5*/s32[]{:T(128)}) while((s32[]{:T(128)}, f32[4,256,128]{2,1,0:T(8,128)S(1)}, s32[]{:T(128)}, f32[32,4,256,128]{3,2,1,0:T(8,128)}, s32[]{:T(128)}, /*index=5*/s32[]{:T(128)}) %tuple.44), condition=%wide.region_2.3_spmd.clone, body=%wide.region_1.2_spmd.clone.sunk | while | flops 393220 | bytes 1572957 | solution.py:17
  118.3 1.2 add_select_fusion.2
  119.5 1.2 add_select_fusion.2
  120.7 1.2 add_select_fusion.2
  122.0 1.2 add_select_fusion.2
  123.2 1.2 add_select_fusion.2
  124.5 1.2 add_select_fusion.2
  125.7 1.2 add_select_fusion.2
  126.9 1.2 add_select_fusion.2
  128.2 1.2 add_select_fusion.2
  129.4 1.2 add_select_fusion.2
  130.7 1.2 add_select_fusion.2
  131.9 1.2 add_select_fusion.2
  155.5 2.2 multiply_reduce_fusion
  159.8 93.4 %all-gather.4.cloned.1.call-done = bf16[1024,4096]{1,0:T(8,128)(2,1)} async-done(((bf16[1024,512]{1,0:T(8,128)(2,1)}), bf16[1024,4096]{1,0:T(8,128)(2,1)}) %all-gather.4.cloned.1.call-update) | async-done | bytes 8388624 | tf_op jit(solution)/shard_map/all_gather | solution.py:66
  253.2 10.0 %convolution_convert_fusion = bf16[1024,512]{1,0:T(8,128)(2,1)} fusion(bf16[1024,4096]{1,0:T(8,128)(2,1)} %all-gather.4.cloned.1.call-done, bf16[4096,512]{1,0:T(8,128)(2,1)} %param.13), kind=kOutput, calls=%fused_computation.23 | convolution fusion | flops 4295491584 | bytes 13631488 | tf_op jit(solution)/shard_map/dot_general | solution.py:65
  (45 shorter events, 26.2 us)
Async XLA Ops:
  6.5 1.9 copy-start
  6.5 1.6 copy-start.2
  6.5 110.5 %all-gather.6.cloned.1.call-start = ((), (), s32[]{:S(2)}) async-start(), calls=%async_computation.1 | async-start | bytes 17301504 | tf_op jit(solution)/shard_map/all_gather | solution.py:10
  18.1 9.8 %copy-start.3 = (bf16[1024,512]{1,0:T(8,128)(2,1)S(1)}, bf16[1024,512]{1,0:T(8,128)(2,1)}, u32[]{:S(2)}) copy-start(bf16[1024,512]{1,0:T(8,128)(2,1)} %param.10) | copy-start | bytes 3145732
  28.2 4.4 %copy-start.4 = (bf16[2,512,4,128]{3,2,1,0:T(4,128)(2,1)}, bf16[2,512,4,128]{3,2,1,0:T(4,128)(2,1)S(1)}, u32[]{:S(2)}) copy-start(bf16[2,512,4,128]{3,2,1,0:T(4,128)(2,1)S(1)} %reshape.36) | copy-start | bytes 3145732
  32.6 2.5 copy-start.1
  35.1 1.5 copy-start.5
  35.2 218.1 %all-gather.4.cloned.1.call-start = ((), (), s32[]{:S(2)}) async-start(), calls=%async_computation | async-start | bytes 9437184 | tf_op jit(solution)/shard_map/all_gather | solution.py:66
Sparse Core Ops, SparseCore 0:
  35.3 81.7 all-gather.5
  160.0 93.2 all-gather.3
where the time goes:
time: 272 us; the launch traced here: 270 us
  waiting for transfers between devices  168 us (62%)
  other arithmetic  43.8 us (16%)
  matrix products  40 us (15%)
  between operations  13.6 us (5%)
  local copies, waits for them, and re-layouts  4.07 us (1%)
    all_gather x1, waiting for transfers between devices, local(): lax.all_gather(normed, 'head', axis=1, tiled=True)  93.4 us
    all_gather x1, waiting for transfers between devices, carried_in(): pieces = lax.all_gather(value, axis)  74.5 us
    select_n x31, other arithmetic, turn(): return jnp.where(position < mine, longer, subtotal)  37.7 us
    dot_general x2, matrix products, features_of(): jnp.einsum('bthd,hdf->bthf', inputs, frequencies, preferred_element_type=...  19.5 us
    dot_general x1, matrix products, local(): jnp.dot(lax.all_gather(normed, 'head', axis=1, tiled=True), out_weight, p...  10 us
    dot_general x1, matrix products, local(): jnp.einsum('bhts,bshd->bthd', scores, value_spans, preferred_element_type...  5.83 us
  transfers between devices with their start and end apart: 2, of which 2 were waited for; matrix products, arithmetic and copies ran while one was open for 3% of the time, Pallas kernels for 0%

commit v1 on v0

--- a/solution.py
+++ b/solution.py
@@ -63,7 +63,9 @@
     )
     normed = normed.reshape(row_count, heads_here * head_width)
     projected = jnp.dot(
-        lax.all_gather(normed, "head", axis=1, tiled=True),
+        jnp.concatenate(
+            lax.all_to_all(jnp.stack([normed] * lax.axis_size("head")), "head", 0, 0), axis=1
+        ),
         out_weight,
         preferred_element_type=jnp.float32,
     )

time: 272 us -> 369 us (1.36)
  blocking collectives: 0 us -> 193 us
  waiting for transfers between devices: 168 us -> 74.6 us
  matrix products: 40 us -> 35.4 us
    all_to_all x0 -> x1, blocking collectives: none -> 193 us  [local(): lax.all_to_all(jnp.stack([normed] * lax.axis_size('head')), 'head', 0, 0)]
    all_gather x1 -> x0, waiting for transfers between devices: 93.4 us -> none  [local(): lax.all_gather(normed, 'head', axis=1, tiled=True)]
    dot_general x1, matrix products: 10 us -> 5.49 us  [local(): jnp.dot(jnp.concatenate(lax.all_to_all(jnp.stack([normed] * lax.axis_size...]
  transfers between devices with their start and end apart: 2 -> 1, of which waited for: 2 -> 1; matrix products, arithmetic and copies ran while one was open for 3% -> 2% of each run, Pallas kernels for 0% -> 0%
where the time goes in v1:
time: 369 us; the launch traced here: 367 us
  blocking collectives  193 us (52%)
  waiting for transfers between devices  74.6 us (20%)
  other arithmetic  43.5 us (12%)
  matrix products  35.4 us (10%)
  between operations  13.6 us (4%)
  local copies, waits for them, and re-layouts  6.26 us (2%)
    all_to_all x1, blocking collectives, local(): lax.all_to_all(jnp.stack([normed] * lax.axis_size('head')), 'head', 0, 0)  193 us
    all_gather x1, waiting for transfers between devices, carried_in(): pieces = lax.all_gather(value, axis)  74.6 us
    select_n x31, other arithmetic, turn(): return jnp.where(position < mine, longer, subtotal)  37.7 us
    dot_general x2, matrix products, features_of(): jnp.einsum('bthd,hdf->bthf', inputs, frequencies, preferred_element_type=...  19.4 us
  transfers between devices with their start and end apart: 1, of which 1 were waited for; matrix products, arithmetic and copies ran while one was open for 2% of the time, Pallas kernels for 0%

profile of v1, /device:TPU:1, one launch (start us, length us, event | category | flops | bytes accessed | tf_op | source)
XLA Modules:
  0.0 366.9 jit_solution(18034599964499348434)
XLA Ops:
  6.5 1.4 reshape.39
  7.9 1.3 reshape.40
  9.3 9.7 %cosine_bitcast_fusion.1 = (f32[2,512,4,128]{1,3,0,2:T(8,128)}, f32[2,512,4,128]{1,3,0,2:T(8,128)}) fusion(bf16[2,512,4,128]{3,2,1,0:T(4,128)(2,1)S(1)} %reshape.39, bf16[4,128,128]{2,1,0:T(8,128)(2,1)S(1)} %copy-done), kind=kOutput, calls=%fused_computation.16 | convolution fusion | flops 134217728 | bytes 5373952 | tf_op jit(solution)/shard_map/bthd,hdf->bthf/dot_general | solution.py:21
  19.0 9.7 %cosine_bitcast_fusion = (f32[2,512,4,128]{1,3,0,2:T(8,128)}, f32[2,512,4,128]{1,3,0,2:T(8,128)}) fusion(bf16[2,512,4,128]{3,2,1,0:T(4,128)(2,1)S(1)} %reshape.40, bf16[4,128,128]{2,1,0:T(8,128)(2,1)S(1)} %copy-done), kind=kOutput, calls=%fused_computation.14 | convolution fusion | flops 134217728 | bytes 5373952 | tf_op jit(solution)/shard_map/bthd,hdf->bthf/dot_general | solution.py:21
  29.8 4.1 %fusion.1 = (bf16[2,512,4,256]{1,3,0,2:T(8,128)(2,1)S(1)}, bf16[2,512,4,256]{1,3,0,2:T(8,128)(2,1)S(1)}) fusion(f32[2,512,4,128]{1,3,0,2:T(8,128)} %get-tuple-element.109, f32[2,512,4,128]{1,3,0,2:T(8,128)} %get-tuple-element.108, f32[2,512,4,128]{1,3,0,2:T(8,128)} %get-tuple-element.111, f32[2,512,4,128]{1,3,0,2:T(8,128)} %get-tuple-element.110), kind=kLoop, calls=%fused_computation.4 | loop fusion | flops 6291456 | bytes 12582912 | tf_op jit(solution)/shard_map/convert_element_type | solution.py:23
  34.0 2.5 fusion.28
  36.5 1.3 fusion.37
  38.0 5.8 %fusion = f32[2,4,512,128]{2,3,1,0:T(8,128)} fusion(pred[512,512]{1,0:T(8,128)(4,1)S(1)} %iota_compare_fusion, bf16[2,512,4,256]{1,3,0,2:T(8,128)(2,1)} %copy-done.2, bf16[2,512,4,256]{1,3,0,2:T(8,128)(2,1)S(1)} %get-tuple-element.116, bf16[2,512,4,128]{3,2,1,0:T(4,128)(2,1)} %reshape.41), kind=kOutput, calls=%fused_computation.2 | convolution fusion | flops 1614807040 | bytes 7602176 | tf_op jit(solution)/shard_map/bhts,bshd->bthd/dot_general | solution.py:52
  43.8 74.6 %all-gather.3.cloned.1.call-done = f32[128,256,128]{2,1,0:T(8,128)} async-done(((f32[4,256,128]{2,1,0:T(8,128)}), f32[128,256,128]{2,1,0:T(8,128)}) %all-gather.3.cloned.1.call-update) | async-done | bytes 16777232 | tf_op jit(solution)/shard_map/all_gather | solution.py:10
  118.4 38.4 %while.14 = (s32[]{:T(128)}, f32[4,256,128]{2,1,0:T(8,128)S(1)}, s32[]{:T(128)}, f32[32,4,256,128]{3,2,1,0:T(8,128)}, s32[]{:T(128)}, /*index=5*/s32[]{:T(128)}) while((s32[]{:T(128)}, f32[4,256,128]{2,1,0:T(8,128)S(1)}, s32[]{:T(128)}, f32[32,4,256,128]{3,2,1,0:T(8,128)}, s32[]{:T(128)}, /*index=5*/s32[]{:T(128)}) %tuple.42), condition=%wide.region_2.3_spmd.clone, body=%wide.region_1.2_spmd.clone.sunk | while | flops 393220 | bytes 1572957 | solution.py:17
  119.6 1.2 add_select_fusion.2
  120.8 1.2 add_select_fusion.2
  122.1 1.2 add_select_fusion.2
  123.3 1.2 add_select_fusion.2
  124.6 1.2 add_select_fusion.2
  125.8 1.2 add_select_fusion.2
  127.0 1.2 add_select_fusion.2
  128.3 1.2 add_select_fusion.2
  129.5 1.2 add_select_fusion.2
  130.8 1.2 add_select_fusion.2
  132.0 1.2 add_select_fusion.2
  156.8 2.2 multiply_reduce_fusion
  161.7 192.9 %all_to_all.5 = bf16[8,1024,512]{1,2,0:T(8,128)(2,1)S(1)} all-to-all(bf16[8,1024,512]{1,2,0:T(8,128)(2,1)S(1)} %stack.3), channel_id=1, replica_groups=mesh['ctx'=32,'head'=8] {'head'}, dimensions={0} | all-to-all | bytes 16777216 | tf_op jit(solution)/shard_map/all_to_all | solution.py:67
  354.5 5.5 %convolution_convert_fusion = bf16[1024,512]{1,0:T(8,128)(2,1)} fusion(bf16[1024,4096]{0,1:T(8,128)(2,1)S(1)} %bitcast.43, bf16[4096,512]{1,0:T(8,128)(2,1)S(1)} %copy-done.6), kind=kOutput, calls=%fused_computation.23 | convolution fusion | flops 4295491584 | bytes 13631488 | tf_op jit(solution)/shard_map/dot_general | solution.py:65
  (46 shorter events, 28.2 us)
Async XLA Ops:
  6.5 2.7 copy-start
  6.5 111.8 %all-gather.3.cloned.1.call-start = ((), (), s32[]{:S(2)}) async-start(), calls=%async_computation.1 | async-start | bytes 17301504 | tf_op jit(solution)/shard_map/all_gather | solution.py:10
  19.0 9.7 %copy-start.3 = (bf16[1024,512]{1,0:T(8,128)(2,1)S(1)}, bf16[1024,512]{1,0:T(8,128)(2,1)}, u32[]{:S(2)}) copy-start(bf16[1024,512]{1,0:T(8,128)(2,1)} %param.10) | copy-start | bytes 3145732
  29.8 4.1 %copy-start.4 = (bf16[2,512,4,128]{3,2,1,0:T(4,128)(2,1)S(1)}, bf16[2,512,4,128]{3,2,1,0:T(4,128)(2,1)}, u32[]{:S(2)}) copy-start(bf16[2,512,4,128]{3,2,1,0:T(4,128)(2,1)} %reshape.41) | copy-start | bytes 3145732
  33.9 2.5 copy-start.2
  36.5 1.5 copy-start.5
  161.7 192.9 %copy-start.6 = (bf16[4096,512]{1,0:T(8,128)(2,1)S(1)}, bf16[4096,512]{1,0:T(8,128)(2,1)}, u32[]{:S(2)}) copy-start(bf16[4096,512]{1,0:T(8,128)(2,1)} %param.13) | copy-start | bytes 12582916
  354.5 5.5 %copy-start.1 = (bf16[4,128,128]{2,1,0:T(8,128)(2,1)S(1)}, bf16[4,128,128]{2,1,0:T(8,128)(2,1)}, u32[]{:S(2)}) copy-start(bf16[4,128,128]{2,1,0:T(8,128)(2,1)} %param.11) | copy-start | bytes 393220
Sparse Core Ops, SparseCore 0:
  36.6 81.7 all-gather.2
